TPU v7x, 512 devices: a whole 4x8x8 slice. The times are simulated.
512 devices in a mesh: band: 8 (over z_hi, core), gx: 8 (over x, z_lo), gy: 8 (over y).
Axes of the slice: x: 4, y: 8, z: 8 (z_hi: 4, z_lo: 2; z = z_hi * 2 + z_lo), core: 2. Of those that a mesh axis runs over, the one named last changes fastest.
Arguments:
- start_bands: float32 [64, 48, 64, 128], P('band', 'gx', 'gy'), may hold values from -40 to 40
- potential: float32 [48, 64, 128], P('gx', 'gy'), may hold values from 0 to 2
Outputs:
- new_bands: float32 [64, 48, 64, 128], P('band', 'gx', 'gy')
All inputs are finite; a program needn't handle non-finite values.
Results may differ from a plain program's by a relative error of at most 0.00025.
Values sent between devices are 32-bit elements; how exact they have to be, the bound alone decides.
A program may use at most 64 MiB of HBM per device.

v0:
```python
import jax
import jax.numpy as jnp
from jax import lax
from jax.sharding import PartitionSpec as P

DEGREE = 4


COEFFS = (
    -5369.0 / 1800.0,
    12.0 / 7.0,
    -15.0 / 56.0,
    10.0 / 189.0,
    -1.0 / 112.0,
    2.0 / 1925.0,
    -1.0 / 16632.0,
)
LOWER_END = -0.5
CUT_LOW = 3.0
CUT_HIGH = 12.7


def padded_2(block, sides, width):
    for axis, dim in sides:
        count = lax.axis_size(axis)
        forward = [(i, i + 1) for i in range(count - 1)]
        forward.append((count - 1, 0))
        backward = [(target, source) for source, target in forward]
        low = lax.ppermute(
            lax.slice_in_dim(block, block.shape[dim] - width, None, axis=dim), axis, forward
        )
        high = lax.ppermute(lax.slice_in_dim(block, 0, width, axis=dim), axis, backward)
        block = jnp.concatenate([low, block, high], axis=dim)
    return block


def filter_weights(degree):
    half_width = (CUT_HIGH - CUT_LOW) / 2.0
    middle = (CUT_HIGH + CUT_LOW) / 2.0
    sigma = half_width / (LOWER_END - middle)
    tau = 2.0 / sigma
    first = sigma / half_width
    others = []
    for index in range(degree - 1):
        sigma_new = 1.0 / (tau - sigma)
        others.append((2.0 * sigma_new / half_width, sigma * sigma_new))
        sigma = sigma_new
    return (middle, first, others)


def hamiltonian(field, potential):
    reach = len(COEFFS) - 1
    width_x = field.shape[1]
    width_y = field.shape[2]
    padded = padded_2(field, (("gx", 1), ("gy", 2)), reach)
    laplace = 3.0 * COEFFS[0] * field
    for offset in range(1, reach + 1):
        ahead_x = padded[:, reach + offset : reach + offset + width_x, reach : reach + width_y]
        behind_x = padded[:, reach - offset : reach - offset + width_x, reach : reach + width_y]
        ahead_y = padded[:, reach : reach + width_x, reach + offset : reach + offset + width_y]
        behind_y = padded[:, reach : reach + width_x, reach - offset : reach - offset + width_y]
        neighbours = ahead_x + behind_x
        neighbours = neighbours + ahead_y + behind_y
        neighbours = neighbours + jnp.roll(field, -offset, 3) + jnp.roll(field, offset, 3)
        laplace = laplace + COEFFS[offset] * neighbours
    return -0.5 * laplace + potential * field


def chebyshev(field, potential):
    middle, first, others = filter_weights(DEGREE)
    current = (hamiltonian(field, potential) - middle * field) * first
    previous = field
    for scale_now, scale_back in others:
        following = (
            hamiltonian(current, potential) - middle * current
        ) * scale_now - scale_back * previous
        previous = current
        current = following
    return current


def invert_factor(margin, identity):
    lower_factor = jnp.linalg.cholesky(margin)
    return jax.scipy.linalg.solve_triangular(lower_factor, identity, lower=True)


def on_device(start_bands, potential):
    filtered = chebyshev(start_bands, potential)
    own_bands = filtered.shape[0]
    flattened = filtered.reshape(own_bands, -1)
    total_cells = flattened.shape[1] * lax.axis_size("gx") * lax.axis_size("gy")
    all_bands = own_bands * lax.axis_size("band")
    identity = jnp.eye(all_bands, dtype=jnp.float32)
    products = jnp.dot(
        flattened,
        lax.all_gather(flattened, "band", axis=0, tiled=True).T,
        precision=lax.Precision.HIGHEST,
        preferred_element_type=jnp.float32,
    )
    first_row = lax.axis_index("band") * own_bands
    summed = lax.psum(products, ("gx", "gy"))
    margin = lax.all_gather(summed, "band", axis=0, tiled=True) * (1.0 / total_cells)
    inverse = invert_factor(margin, identity)
    own_rows = lax.dynamic_slice_in_dim(inverse, first_row, own_bands, 0)
    rotated = jnp.dot(
        own_rows,
        lax.all_gather(flattened, "band", axis=0, tiled=True),
        precision=lax.Precision.HIGHEST,
        preferred_element_type=jnp.float32,
    )
    return rotated.reshape(filtered.shape)


def solution(mesh):
    in_specs = (P("band", "gx", "gy", None), P("gx", "gy", None))
    out_specs = P("band", "gx", "gy", None)
    return jax.shard_map(
        on_device, mesh=mesh, in_specs=in_specs, out_specs=out_specs, check_vma=False
    )
```

profile of v0, /device:TPU:1, one launch (start us, length us, event | category | flops | bytes accessed | tf_op | source)
XLA Modules:
  0.0 359.3 jit_solution(18137484880610322093)
XLA Ops:
  6.5 1.0 copy.6
  7.5 4.8 %collective-permute-start.1 = (f32[8,6,8,128]{3,0,2,1:T(8,128)S(1)}, f32[8,6,8,128]{3,0,2,1:T(8,128)S(1)}, u32[]{:S(2)}, u32[]{:S(2)}) collective-permute-start(f32[8,6,8,128]{3,0,2,1:T(8,128)S(1)} %copy.6), channel_id=1, source_target_pairs={{0,8},{8,16},{16,24},{24,32},{32,40},{40,48},{48,56},{56,0},{1,9},... | collective-permute-start | bytes 589832 | tf_op jit(solution)/shard_map/ppermute | solution.py:29
  12.4 4.1 %collective-permute-start = (f32[8,6,8,128]{3,0,2,1:T(8,128)S(1)}, f32[8,6,8,128]{3,0,2,1:T(8,128)S(1)}, u32[]{:S(2)}, u32[]{:S(2)}) collective-permute-start(f32[8,6,8,128]{3,0,2,1:T(8,128)S(1)} %copy.6), channel_id=1, source_target_pairs={{8,0},{16,8},{24,16},{32,24},{40,32},{48,40},{56,48},{0,56},{9,1},... | collective-permute-start | bytes 589832 | tf_op jit(solution)/shard_map/ppermute | solution.py:32
  17.9 0.5 copy-done.1
  18.5 2.7 collective-permute-done
  21.3 5.1 %collective-permute-start.2 = (f32[8,18,6,128]{3,0,2,1:T(8,128)S(1)}, f32[8,18,6,128]{3,0,2,1:T(8,128)S(1)}, u32[]{:S(2)}, u32[]{:S(2)}) collective-permute-start(f32[8,18,6,128]{3,0,2,1:T(8,128)S(1)} %get-tuple-element.19), channel_id=1, source_target_pairs={{1,0},{2,1},{3,2},{4,3},{5,4},{6,5},{7,6},{0,7},{9,8},{10,9},{11,1... | collective-permute-start | bytes 1327112 | tf_op jit(solution)/shard_map/ppermute | solution.py:32
  26.4 1.9 collective-permute-start.3
  28.5 5.9 %collective-permute-done.2 = f32[8,18,6,128]{3,0,2,1:T(8,128)S(1)} collective-permute-done((f32[8,18,6,128]{3,0,2,1:T(8,128)S(1)}, f32[8,18,6,128]{3,0,2,1:T(8,128)S(1)}, u32[]{:S(2)}, u32[]{:S(2)}) %collective-permute-start.2) | collective-permute-done | bytes 442400 | tf_op jit(solution)/shard_map/ppermute | solution.py:32
  34.4 5.0 %collective-permute-done.3 = f32[8,18,6,128]{3,0,2,1:T(8,128)S(1)} collective-permute-done((f32[8,18,6,128]{3,0,2,1:T(8,128)S(1)}, f32[8,18,6,128]{3,0,2,1:T(8,128)S(1)}, u32[]{:S(2)}, u32[]{:S(2)}) %collective-permute-start.3) | collective-permute-done | bytes 442400 | tf_op jit(solution)/shard_map/ppermute | solution.py:29
  39.4 1.0 broadcast_multiply_fusion
  40.4 5.0 %collective-permute-start.4 = (f32[8,6,8,128]{3,0,2,1:T(8,128)S(1)}, f32[8,6,8,128]{3,0,2,1:T(8,128)S(1)}, u32[]{:S(2)}, u32[]{:S(2)}) collective-permute-start(f32[8,6,8,128]{3,0,2,1:T(8,128)S(1)} %get-tuple-element.5), channel_id=1, source_target_pairs={{8,0},{16,8},{24,16},{32,24},{40,32},{48,40},{56,48},{0,56},{9,1},... | collective-permute-start | bytes 589832 | tf_op jit(solution)/shard_map/ppermute | solution.py:32
  45.4 1.9 collective-permute-start.5
  48.6 5.7 %collective-permute-done.5 = f32[8,6,8,128]{3,0,2,1:T(8,128)S(1)} collective-permute-done((f32[8,6,8,128]{3,0,2,1:T(8,128)S(1)}, f32[8,6,8,128]{3,0,2,1:T(8,128)S(1)}, u32[]{:S(2)}, u32[]{:S(2)}) %collective-permute-start.5) | collective-permute-done | bytes 196640 | tf_op jit(solution)/shard_map/ppermute | solution.py:29
  54.4 1.9 collective-permute-start.6
  56.3 3.4 collective-permute-start.7
  59.9 4.0 %collective-permute-done.6 = f32[8,18,6,128]{3,0,2,1:T(8,128)S(1)} collective-permute-done((f32[8,18,6,128]{3,0,2,1:T(8,128)S(1)}, f32[8,18,6,128]{3,0,2,1:T(8,128)S(1)}, u32[]{:S(2)}, u32[]{:S(2)}) %collective-permute-start.6) | collective-permute-done | bytes 442400 | tf_op jit(solution)/shard_map/ppermute | solution.py:32
  63.9 3.0 collective-permute-done.7
  67.0 0.2 pad_maximum_fusion
  67.1 1.1 fusion.100
  68.2 2.8 collective-permute-start.8
  71.0 2.5 collective-permute-start.9
  74.7 5.9 %collective-permute-done.9 = f32[8,6,8,128]{3,0,2,1:T(8,128)S(1)} collective-permute-done((f32[8,6,8,128]{3,0,2,1:T(8,128)S(1)}, f32[8,6,8,128]{3,0,2,1:T(8,128)S(1)}, u32[]{:S(2)}, u32[]{:S(2)}) %collective-permute-start.9) | collective-permute-done | bytes 196640 | tf_op jit(solution)/shard_map/ppermute | solution.py:29
  80.8 1.9 collective-permute-start.10
  82.7 3.4 collective-permute-start.11
  86.3 3.5 collective-permute-done.10
  89.8 3.1 collective-permute-done.11
  93.0 0.2 pad_maximum_fusion.1
  93.1 1.0 fusion.57
  94.1 1.9 collective-permute-start.12
  96.0 3.4 collective-permute-start.13
  100.6 4.6 %collective-permute-done.13 = f32[8,6,8,128]{3,0,2,1:T(8,128)S(1)} collective-permute-done((f32[8,6,8,128]{3,0,2,1:T(8,128)S(1)}, f32[8,6,8,128]{3,0,2,1:T(8,128)S(1)}, u32[]{:S(2)}, u32[]{:S(2)}) %collective-permute-start.13) | collective-permute-done | bytes 196640 | tf_op jit(solution)/shard_map/ppermute | solution.py:29
  105.4 1.9 collective-permute-start.14
  107.3 3.4 collective-permute-start.15
  110.9 3.5 collective-permute-done.14
  114.4 3.1 collective-permute-done.15
  117.5 0.2 pad_maximum_fusion.2
  117.7 1.7 fusion.14
  119.4 42.7 %all-gather.2.cloned.1.call-done = f32[64,6144]{1,0:T(8,128)} async-done(((f32[8,6144]{1,0:T(8,128)}), f32[64,6144]{1,0:T(8,128)}) %all-gather.2.cloned.1.call-update) | async-done | bytes 1572880 | tf_op jit(solution)/shard_map/all_gather | solution.py:96
  162.1 2.9 fusion.259
  165.1 130.7 %psum.7 = f32[8,64]{1,0:T(8,128)S(1)} all-reduce(f32[8,64]{1,0:T(8,128)S(1)} %fusion.259), channel_id=1, replica_groups=mesh['band'=8,'gx'=8,'gy'=8] {'gx','gy'}, use_global_device_ids=true, to_apply=%region_0.1 | all-reduce | flops 512 | bytes 4096 | tf_op jit(solution)/shard_map/psum | solution.py:101
  295.8 42.6 %all_gather.8 = f32[64,64]{1,0:T(8,128)S(1)} all-gather(f32[8,64]{1,0:T(8,128)S(1)} %psum.7), channel_id=1, replica_groups=mesh['band'=8,'gx'=8,'gy'=8] {'band'}, dimensions={0}, use_global_device_ids=true | all-gather | bytes 18432 | tf_op jit(solution)/shard_map/all_gather | solution.py:102
  338.6 5.8 %cholesky.17 = f32[64,64]{1,0:T(8,128)S(1)} custom-call(f32[64,64]{1,0:T(8,128)S(1)} %fusion.202), custom_call_target="Cholesky" | custom-call | tf_op jit(solution)/shard_map/jit(cholesky)/cholesky | solution.py:83
  344.5 0.6 compare_reduce_fusion
  345.1 0.7 fusion.199
  345.8 4.9 %custom-call.7 = f32[1,64,64]{1,2,0:T(8,128)S(1)} custom-call(f32[1,64,64]{2,1,0:T(8,128)S(1)} %fusion.199), custom_call_target="InvertDiagBlocksLowerTriangular" | custom-call | tf_op jit(solution)/shard_map/jit(_solve_triangular)/triangular_solve | solution.py:84
  350.7 0.2 fusion.200
  350.9 0.8 fusion.203
  351.8 0.7 copy.41
  (75 shorter events, 6.2 us)
Async XLA Ops:
  6.5 155.6 %all-gather.2.cloned.1.call-start = ((), (), s32[]{:S(2)}) async-start(), calls=%async_computation | async-start | bytes 1769472 | tf_op jit(solution)/shard_map/all_gather | solution.py:96
  7.5 10.3 %collective-permute-start.1 = (f32[8,6,8,128]{3,0,2,1:T(8,128)S(1)}, f32[8,6,8,128]{3,0,2,1:T(8,128)S(1)}, u32[]{:S(2)}, u32[]{:S(2)}) collective-permute-start(f32[8,6,8,128]{3,0,2,1:T(8,128)S(1)} %copy.6), channel_id=1, source_target_pairs={{0,8},{8,16},{16,24},{24,32},{32,40},{40,48},{48,56},{56,0},{1,9},... | collective-permute-start | bytes 589832 | tf_op jit(solution)/shard_map/ppermute | solution.py:29
  12.4 8.8 %collective-permute-start = (f32[8,6,8,128]{3,0,2,1:T(8,128)S(1)}, f32[8,6,8,128]{3,0,2,1:T(8,128)S(1)}, u32[]{:S(2)}, u32[]{:S(2)}) collective-permute-start(f32[8,6,8,128]{3,0,2,1:T(8,128)S(1)} %copy.6), channel_id=1, source_target_pairs={{8,0},{16,8},{24,16},{32,24},{40,32},{48,40},{56,48},{0,56},{9,1},... | collective-permute-start | bytes 589832 | tf_op jit(solution)/shard_map/ppermute | solution.py:32
  17.5 0.9 copy-start.1
  18.4 9.9 %copy-start.2 = (f32[6,8,128]{2,1,0:T(8,128)S(1)}, f32[6,8,128]{2,1,0:T(8,128)}, u32[]{:S(2)}) copy-start(f32[6,8,128]{2,1,0:T(8,128)} %param.3) | copy-start | bytes 73732
  21.3 13.1 %collective-permute-start.2 = (f32[8,18,6,128]{3,0,2,1:T(8,128)S(1)}, f32[8,18,6,128]{3,0,2,1:T(8,128)S(1)}, u32[]{:S(2)}, u32[]{:S(2)}) collective-permute-start(f32[8,18,6,128]{3,0,2,1:T(8,128)S(1)} %get-tuple-element.19), channel_id=1, source_target_pairs={{1,0},{2,1},{3,2},{4,3},{5,4},{6,5},{7,6},{0,7},{9,8},{10,9},{11,1... | collective-permute-start | bytes 1327112 | tf_op jit(solution)/shard_map/ppermute | solution.py:32
  26.4 13.0 %collective-permute-start.3 = (f32[8,18,6,128]{3,0,2,1:T(8,128)S(1)}, f32[8,18,6,128]{3,0,2,1:T(8,128)S(1)}, u32[]{:S(2)}, u32[]{:S(2)}) collective-permute-start(f32[8,18,6,128]{3,0,2,1:T(8,128)S(1)} %get-tuple-element.20), channel_id=1, source_target_pairs={{0,1},{1,2},{2,3},{3,4},{4,5},{5,6},{6,7},{7,0},{8,9},{9,10},{10,1... | collective-permute-start | bytes 1327112 | tf_op jit(solution)/shard_map/ppermute | solution.py:29
  40.4 8.1 %collective-permute-start.4 = (f32[8,6,8,128]{3,0,2,1:T(8,128)S(1)}, f32[8,6,8,128]{3,0,2,1:T(8,128)S(1)}, u32[]{:S(2)}, u32[]{:S(2)}) collective-permute-start(f32[8,6,8,128]{3,0,2,1:T(8,128)S(1)} %get-tuple-element.5), channel_id=1, source_target_pairs={{8,0},{16,8},{24,16},{32,24},{40,32},{48,40},{56,48},{0,56},{9,1},... | collective-permute-start | bytes 589832 | tf_op jit(solution)/shard_map/ppermute | solution.py:32
  45.4 8.9 %collective-permute-start.5 = (f32[8,6,8,128]{3,0,2,1:T(8,128)S(1)}, f32[8,6,8,128]{3,0,2,1:T(8,128)S(1)}, u32[]{:S(2)}, u32[]{:S(2)}) collective-permute-start(f32[8,6,8,128]{3,0,2,1:T(8,128)S(1)} %get-tuple-element.5), channel_id=1, source_target_pairs={{0,8},{8,16},{16,24},{24,32},{32,40},{40,48},{48,56},{56,0},{1,9},... | collective-permute-start | bytes 589832 | tf_op jit(solution)/shard_map/ppermute | solution.py:29
  54.4 9.6 %collective-permute-start.6 = (f32[8,18,6,128]{3,0,2,1:T(8,128)S(1)}, f32[8,18,6,128]{3,0,2,1:T(8,128)S(1)}, u32[]{:S(2)}, u32[]{:S(2)}) collective-permute-start(f32[8,18,6,128]{3,0,2,1:T(8,128)S(1)} %get-tuple-element.17), channel_id=1, source_target_pairs={{1,0},{2,1},{3,2},{4,3},{5,4},{6,5},{7,6},{0,7},{9,8},{10,9},{11,1... | collective-permute-start | bytes 1327112 | tf_op jit(solution)/shard_map/ppermute | solution.py:32
  56.3 10.7 %collective-permute-start.7 = (f32[8,18,6,128]{3,0,2,1:T(8,128)S(1)}, f32[8,18,6,128]{3,0,2,1:T(8,128)S(1)}, u32[]{:S(2)}, u32[]{:S(2)}) collective-permute-start(f32[8,18,6,128]{3,0,2,1:T(8,128)S(1)} %get-tuple-element.18), channel_id=1, source_target_pairs={{0,1},{1,2},{2,3},{3,4},{4,5},{5,6},{6,7},{7,0},{8,9},{9,10},{10,1... | collective-permute-start | bytes 1327112 | tf_op jit(solution)/shard_map/ppermute | solution.py:29
  68.2 6.5 %collective-permute-start.8 = (f32[8,6,8,128]{3,0,2,1:T(8,128)S(1)}, f32[8,6,8,128]{3,0,2,1:T(8,128)S(1)}, u32[]{:S(2)}, u32[]{:S(2)}) collective-permute-start(f32[8,6,8,128]{3,0,2,1:T(8,128)S(1)} %fusion.100), channel_id=1, source_target_pairs={{8,0},{16,8},{24,16},{32,24},{40,32},{48,40},{56,48},{0,56},{9,1},... | collective-permute-start | bytes 589832 | tf_op jit(solution)/shard_map/ppermute | solution.py:32
  71.0 9.7 %collective-permute-start.9 = (f32[8,6,8,128]{3,0,2,1:T(8,128)S(1)}, f32[8,6,8,128]{3,0,2,1:T(8,128)S(1)}, u32[]{:S(2)}, u32[]{:S(2)}) collective-permute-start(f32[8,6,8,128]{3,0,2,1:T(8,128)S(1)} %fusion.100), channel_id=1, source_target_pairs={{0,8},{8,16},{16,24},{24,32},{32,40},{40,48},{48,56},{56,0},{1,9},... | collective-permute-start | bytes 589832 | tf_op jit(solution)/shard_map/ppermute | solution.py:29
  80.8 9.0 %collective-permute-start.10 = (f32[8,18,6,128]{3,0,2,1:T(8,128)S(1)}, f32[8,18,6,128]{3,0,2,1:T(8,128)S(1)}, u32[]{:S(2)}, u32[]{:S(2)}) collective-permute-start(f32[8,18,6,128]{3,0,2,1:T(8,128)S(1)} %get-tuple-element.13), channel_id=1, source_target_pairs={{1,0},{2,1},{3,2},{4,3},{5,4},{6,5},{7,6},{0,7},{9,8},{10,9},{11,1... | collective-permute-start | bytes 1327112 | tf_op jit(solution)/shard_map/ppermute | solution.py:32
  82.7 10.3 %collective-permute-start.11 = (f32[8,18,6,128]{3,0,2,1:T(8,128)S(1)}, f32[8,18,6,128]{3,0,2,1:T(8,128)S(1)}, u32[]{:S(2)}, u32[]{:S(2)}) collective-permute-start(f32[8,18,6,128]{3,0,2,1:T(8,128)S(1)} %get-tuple-element.14), channel_id=1, source_target_pairs={{0,1},{1,2},{2,3},{3,4},{4,5},{5,6},{6,7},{7,0},{8,9},{9,10},{10,1... | collective-permute-start | bytes 1327112 | tf_op jit(solution)/shard_map/ppermute | solution.py:29
  94.1 6.5 %collective-permute-start.12 = (f32[8,6,8,128]{3,0,2,1:T(8,128)S(1)}, f32[8,6,8,128]{3,0,2,1:T(8,128)S(1)}, u32[]{:S(2)}, u32[]{:S(2)}) collective-permute-start(f32[8,6,8,128]{3,0,2,1:T(8,128)S(1)} %fusion.57), channel_id=1, source_target_pairs={{8,0},{16,8},{24,16},{32,24},{40,32},{48,40},{56,48},{0,56},{9,1},... | collective-permute-start | bytes 589832 | tf_op jit(solution)/shard_map/ppermute | solution.py:32
  96.0 9.2 %collective-permute-start.13 = (f32[8,6,8,128]{3,0,2,1:T(8,128)S(1)}, f32[8,6,8,128]{3,0,2,1:T(8,128)S(1)}, u32[]{:S(2)}, u32[]{:S(2)}) collective-permute-start(f32[8,6,8,128]{3,0,2,1:T(8,128)S(1)} %fusion.57), channel_id=1, source_target_pairs={{0,8},{8,16},{16,24},{24,32},{32,40},{40,48},{48,56},{56,0},{1,9},... | collective-permute-start | bytes 589832 | tf_op jit(solution)/shard_map/ppermute | solution.py:29
  105.4 9.0 %collective-permute-start.14 = (f32[8,18,6,128]{3,0,2,1:T(8,128)S(1)}, f32[8,18,6,128]{3,0,2,1:T(8,128)S(1)}, u32[]{:S(2)}, u32[]{:S(2)}) collective-permute-start(f32[8,18,6,128]{3,0,2,1:T(8,128)S(1)} %get-tuple-element.9), channel_id=1, source_target_pairs={{1,0},{2,1},{3,2},{4,3},{5,4},{6,5},{7,6},{0,7},{9,8},{10,9},{11,1... | collective-permute-start | bytes 1327112 | tf_op jit(solution)/shard_map/ppermute | solution.py:32
  107.3 10.3 %collective-permute-start.15 = (f32[8,18,6,128]{3,0,2,1:T(8,128)S(1)}, f32[8,18,6,128]{3,0,2,1:T(8,128)S(1)}, u32[]{:S(2)}, u32[]{:S(2)}) collective-permute-start(f32[8,18,6,128]{3,0,2,1:T(8,128)S(1)} %get-tuple-element.10), channel_id=1, source_target_pairs={{0,1},{1,2},{2,3},{3,4},{4,5},{5,6},{6,7},{7,0},{8,9},{9,10},{10,1... | collective-permute-start | bytes 1327112 | tf_op jit(solution)/shard_map/ppermute | solution.py:29
  162.1 188.8 %copy-start = (f32[64,6144]{1,0:T(8,128)S(1)}, f32[64,6144]{1,0:T(8,128)}, u32[]{:S(2)}) copy-start(f32[64,6144]{1,0:T(8,128)} %all-gather.2.cloned.1.call-done) | copy-start | bytes 4718596
Sparse Core Ops, SparseCore 0:
  119.5 42.5 all-gather.1
where the time goes:
time: 360 us; the launch traced here: 359 us
  blocking collectives  173 us (48%)
  waiting for transfers between devices  93 us (26%)
  starting transfers between devices  49.3 us (14%)
  other arithmetic  17.4 us (5%)
  between operations  14.1 us (4%)
  local copies, waits for them, and re-layouts  8.21 us (2%)
  matrix products  4.01 us (1%)
    psum x1, blocking collectives, on_device(): summed = lax.psum(products, ('gx', 'gy'))  131 us
    all_gather x1, waiting for transfers between devices, on_device(): lax.all_gather(flattened, 'band', axis=0, tiled=True)  42.7 us
    all_gather x1, blocking collectives, on_device(): lax.all_gather(summed, 'band', axis=0, tiled=True) * (1.0 / total_cells)  42.6 us
    ppermute x8, waiting for transfers between devices, padded_2(): lax.ppermute(lax.slice_in_dim(block, block.shape[dim] - width, None, axis...  30.6 us
    ppermute x8, starting transfers between devices, padded_2(): lax.ppermute(lax.slice_in_dim(block, block.shape[dim] - width, None, axis...  24.6 us
    ppermute x8, starting transfers between devices, padded_2(): lax.ppermute(lax.slice_in_dim(block, 0, width, axis=dim), axis, backward)  24.6 us
    ppermute x8, waiting for transfers between devices, padded_2(): lax.ppermute(lax.slice_in_dim(block, 0, width, axis=dim), axis, backward)  19.7 us
  transfers between devices with their start and end apart: 17, of which 13 were waited for; matrix products, arithmetic and copies ran while one was open for 2% of the time, Pallas kernels for 0%

commit v1 on v0

v1 whole, which is shorter than its diff:
```python
import jax
import jax.numpy as jnp
from jax import lax
from jax.experimental import pallas as pl
from jax.experimental.pallas import tpu as pltpu
from jax.sharding import PartitionSpec as P

DEGREE = 4
COEFFS = (
    -5369.0 / 1800.0,
    12.0 / 7.0,
    -15.0 / 56.0,
    10.0 / 189.0,
    -1.0 / 112.0,
    2.0 / 1925.0,
    -1.0 / 16632.0,
)
LOWER_END = -0.5
CUT_LOW = 3.0
CUT_HIGH = 12.7
REACH = 6
MESH = pl.DeviceIdType.MESH
NB, NG, NY = 8, 8, 8
XW, YW, NX, NZ = 6, 8, 48, 128
BANDS = 64
CELLS = 48 * 64 * 128


def filter_weights(degree):
    half_width = (CUT_HIGH - CUT_LOW) / 2.0
    middle = (CUT_HIGH + CUT_LOW) / 2.0
    sigma = half_width / (LOWER_END - middle)
    tau = 2.0 / sigma
    first = sigma / half_width
    others = []
    for index in range(degree - 1):
        sigma_new = 1.0 / (tau - sigma)
        others.append((2.0 * sigma_new / half_width, sigma * sigma_new))
        sigma = sigma_new
    return (middle, first, others)


def wait_bytes(ref, sem):
    pltpu.make_async_copy(ref, ref, sem).wait()


def dot(a, b, contract):
    return lax.dot_general(
        a,
        b,
        (contract, ((), ())),
        precision=lax.Precision.HIGHEST,
        preferred_element_type=jnp.float32,
    )


def inverse_factor(packed):
    lane = lax.broadcasted_iota(jnp.int32, (8, 128), 1)
    sub = lax.broadcasted_iota(jnp.int32, (8, 128), 0)
    rows = []
    for t in range(8):
        part = packed[8 * (t % 4) : 8 * (t % 4) + 8]
        if t >= 4:
            part = pltpu.roll(part, 64, 1)
        unit = jnp.where(lane == sub + 8 * t, 1.0, 0.0)
        rows.append(jnp.where(lane >= 64, part, unit))
    for k in range(BANDS - 1):
        t, s = divmod(k, 8)
        row = jnp.broadcast_to(rows[t][s : s + 1, :], (8, 128))
        pivot = jnp.broadcast_to(rows[t][s : s + 1, 64 + k : 65 + k], (8, 128))
        scaled = row / pivot
        for i in range(t, 8):
            column = jnp.broadcast_to(rows[i][:, 64 + k : 65 + k], (8, 128))
            if i == t:
                column = jnp.where(sub > s, column, 0.0)
            rows[i] = rows[i] - column * scaled
    done = []
    for t in range(8):
        pivots = jnp.sum(jnp.where(lane == sub + (8 * t + 64), rows[t], 0.0), axis=1, keepdims=True)
        done.append(rows[t] * (1.0 / jnp.sqrt(pivots)))
    return jnp.concatenate(done, axis=0)[:, :BANDS]


def kernel(
    start,
    pot,
    out,
    own,
    own_pot,
    field,
    last,
    pots,
    acc,
    pencil,
    rotated,
    packed,
    half,
    both,
    sum_y,
    sum_z,
    sum_x,
    local_sem,
    ax_send,
    ax_recv,
    pot_send,
    pot_recv,
    first_send,
    first_recv,
    halo_send,
    halo_recv,
    pen_send,
    pen_recv,
    sum_send,
    sum_recv,
    back_send,
    back_recv,
):
    b = lax.axis_index("band")
    g = lax.axis_index("gx")
    r = lax.axis_index("gy")

    def remote(src, dst, send, recv, device):
        copy = pltpu.make_async_remote_copy(
            src_ref=src, dst_ref=dst, send_sem=send, recv_sem=recv, device_id=device, device_id_type=MESH
        )
        copy.start()
        return copy

    load = pltpu.make_async_copy(start, own, local_sem.at[0])
    load.start()
    load_pot = pltpu.make_async_copy(pot, own_pot, local_sem.at[1])
    load_pot.start()

    plane_peers = [(db, dg) for db in range(NB) for dg in range(NG) if db or dg]
    barrier = pltpu.get_barrier_semaphore()
    for db, dg in plane_peers:
        device = {"band": lax.rem(b + db, NB), "gx": lax.rem(g + dg, NG)}
        pl.semaphore_signal(barrier, inc=1, device_id=device, device_id_type=MESH)
    for dy in range(1, NY):
        pl.semaphore_signal(barrier, inc=1, device_id={"gy": lax.rem(r + dy, NY)}, device_id_type=MESH)
    pl.semaphore_wait(barrier, len(plane_peers) + NY - 1)
    load.wait()
    load_pot.wait()

    for dg in range(1, NG):
        to = lax.rem(g + dg, NG)
        for x in range(XW):
            remote(
                own.at[to, x],
                field.at[0, pl.ds(REACH, YW), XW * g + x, :],
                ax_send,
                ax_recv.at[g],
                {"gx": to},
            )
    mine = []
    for x in range(XW):
        copy = pltpu.make_async_copy(
            own.at[g, x], field.at[0, pl.ds(REACH, YW), XW * g + x, :], local_sem.at[2 + x]
        )
        copy.start()
        mine.append(copy)
    for copy in mine:
        copy.wait()

    up = {"gy": lax.rem(r + 1, NY)}
    down = {"gy": lax.rem(r + NY - 1, NY)}

    def forward(index):
        cols = pl.ds(XW * index, XW)
        remote(
            field.at[0, pl.ds(YW, REACH), cols, :],
            field.at[0, pl.ds(0, REACH), cols, :],
            first_send.at[0],
            first_recv.at[0],
            up,
        )
        remote(
            field.at[0, pl.ds(REACH, REACH), cols, :],
            field.at[0, pl.ds(YW + REACH, REACH), cols, :],
            first_send.at[1],
            first_recv.at[1],
            down,
        )

    forward(g)
    for dg in range(1, NG):
        source = lax.rem(g + NG - dg, NG)
        wait_bytes(field.at[0, pl.ds(REACH, YW), pl.ds(XW * source, XW), :], ax_recv.at[source])
        forward(source)
    wait_bytes(own.at[pl.ds(0, NG - 1)], ax_send)

    for dg in range(1, NG):
        to = lax.rem(g + dg, NG)
        for x in range(XW):
            remote(own_pot.at[x], pots.at[:, XW * g + x, :], pot_send, pot_recv, {"gx": to})
    mine = []
    for x in range(XW):
        copy = pltpu.make_async_copy(own_pot.at[x], pots.at[:, XW * g + x, :], local_sem.at[2 + x])
        copy.start()
        mine.append(copy)
    for copy in mine:
        copy.wait()
    wait_bytes(pots.at[:, pl.ds(0, XW * (NG - 1)), :], pot_recv)
    wait_bytes(pots.at[:, pl.ds(0, XW * (NG - 1)), :], pot_send)

    middle, first, others = filter_weights(DEGREE)
    for k in range(DEGREE):
        scale = first if k == 0 else others[k - 1][0]
        weights = [-0.5 * c * scale for c in COEFFS]
        if k:
            moves = [
                remote(
                    field.at[k, pl.ds(YW, REACH)],
                    field.at[k, pl.ds(0, REACH)],
                    halo_send.at[k, 0],
                    halo_recv.at[k, 0],
                    up,
                ),
                remote(
                    field.at[k, pl.ds(REACH, REACH)],
                    field.at[k, pl.ds(YW + REACH, REACH)],
                    halo_send.at[k, 1],
                    halo_recv.at[k, 1],
                    down,
                ),
            ]

        def local_part(y, carry, k=k, scale=scale, weights=weights):
            plane = field[k, REACH + y]
            total = (scale * pots[y] + (3.0 * weights[0] - middle * scale)) * plane
            for j in range(1, REACH + 1):
                near = pltpu.roll(plane, j, 0) + pltpu.roll(plane, NX - j, 0)
                near = near + pltpu.roll(plane, j, 1) + pltpu.roll(plane, NZ - j, 1)
                total = total + weights[j] * near
            if k:
                total = total - others[k - 1][1] * field[k - 1, REACH + y]
            acc[y] = total
            return carry

        lax.fori_loop(0, YW, local_part, 0)
        for y in range(YW):
            total = acc[y]
            for j in range(1, REACH + 1):
                if y - j >= 0:
                    total = total + weights[j] * field[k, REACH + y - j]
                if y + j < YW:
                    total = total + weights[j] * field[k, REACH + y + j]
            acc[y] = total

        if k:
            for move in moves:
                move.wait()
        else:
            for side in range(2):
                low = 0 if side == 0 else YW + REACH
                wait_bytes(field.at[0, pl.ds(low, REACH)], first_recv.at[side])
                wait_bytes(field.at[0, pl.ds(low, REACH)], first_send.at[side])
        for y in range(YW):
            total = acc[y]
            for j in range(1, REACH + 1):
                if y - j < 0:
                    total = total + weights[j] * field[k, REACH + y - j]
                if y + j >= YW:
                    total = total + weights[j] * field[k, REACH + y + j]
            if k < DEGREE - 1:
                field[k + 1, REACH + y] = total
            else:
                last[y] = total

    band = NG * b + g
    for db, dg in plane_peers:
        to_b = lax.rem(b + db, NB)
        to_g = lax.rem(g + dg, NG)
        remote(
            last.at[to_b, pl.ds(XW * to_g, XW), :],
            pencil.at[:, band, :],
            pen_send,
            pen_recv,
            {"band": to_b, "gx": to_g},
        )
    copy = pltpu.make_async_copy(last.at[b, pl.ds(XW * g, XW), :], pencil.at[:, band, :], local_sem.at[0])
    copy.start()
    copy.wait()
    wait_bytes(pencil.at[:, pl.ds(0, BANDS - 1), :], pen_recv)
    wait_bytes(pencil.at[:, pl.ds(0, BANDS - 1), :], pen_send)

    cells = jnp.concatenate([pencil[x] for x in range(XW)], axis=1)
    twice = jnp.concatenate([cells, cells], axis=0)
    products = dot(cells, twice, ((1,), (1,)))
    lane = lax.broadcasted_iota(jnp.int32, (32, 128), 1)
    joined = jnp.where(lane < 64, products[32:], products[:32])
    packed[...] = joined.reshape(2, 16, 128)

    core = lax.rem(b, 2)
    partner = {"band": b + 1 - 2 * core}
    move = remote(packed.at[1 - core], half, sum_send.at[0], sum_recv.at[0], partner)
    move.wait()
    zhi, zlo, chip_x = b // 2, lax.rem(g, 2), g // 2

    def exchange(table, value, slot, peers, stage):
        table[slot] = value
        for device in peers:
            remote(table.at[slot], table.at[slot], sum_send.at[stage], sum_recv.at[stage], device)
        count = len(peers)
        wait_bytes(table.at[pl.ds(0, count)], sum_recv.at[stage])
        wait_bytes(table.at[pl.ds(0, count)], sum_send.at[stage])
        total = table[0]
        for i in range(1, count + 1):
            total = total + table[i]
        return total

    value = packed[core] + half[...]
    value = exchange(sum_y, value, r, [{"gy": lax.rem(r + d, NY)} for d in range(1, NY)], 1)
    place = 2 * zhi + zlo
    peers = []
    for d in range(1, 8):
        other = lax.rem(place + d, 8)
        peers.append({"band": 2 * (other // 2) + core, "gx": 2 * chip_x + lax.rem(other, 2)})
    value = exchange(sum_z, value, place, peers, 2)
    peers = [{"gx": 2 * lax.rem(chip_x + d, 4) + zlo} for d in range(1, 4)]
    value = exchange(sum_x, value, chip_x, peers, 3)
    both[core] = value * (1.0 / CELLS)
    move = remote(both.at[core], both.at[core], sum_send.at[4], sum_recv.at[4], partner)
    move.wait()

    inverse = inverse_factor(both[...].reshape(32, 128))
    for x in range(XW):
        rotated[x] = dot(inverse, pencil[x], ((1,), (0,)))

    for db in range(1, NB):
        to = lax.rem(b + db, NB)
        for x in range(XW):
            remote(
                rotated.at[x, pl.ds(8 * to, 8), :], out.at[:, x, b, :], back_send, back_recv, {"band": to}
            )
    mine = []
    for x in range(XW):
        copy = pltpu.make_async_copy(rotated.at[x, pl.ds(8 * b, 8), :], out.at[:, x, b, :], local_sem.at[2 + x])
        copy.start()
        mine.append(copy)
    for copy in mine:
        copy.wait()
    wait_bytes(own.at[pl.ds(0, NB - 1)], back_recv)
    wait_bytes(own.at[pl.ds(0, NB - 1)], back_send)


def on_device(start_bands, potential):
    f32 = jnp.float32
    dma = pltpu.SemaphoreType.DMA
    return pl.pallas_call(
        kernel,
        out_shape=jax.ShapeDtypeStruct((8, XW, YW, NZ), f32),
        in_specs=[pl.BlockSpec(memory_space=pl.ANY)] * 2,
        out_specs=pl.BlockSpec(memory_space=pl.ANY),
        scratch_shapes=[
            pltpu.VMEM((8, XW, YW, NZ), f32),
            pltpu.VMEM((XW, YW, NZ), f32),
            pltpu.VMEM((DEGREE, YW + 2 * REACH, NX, NZ), f32),
            pltpu.VMEM((YW, NX, NZ), f32),
            pltpu.VMEM((YW, NX, NZ), f32),
            pltpu.VMEM((YW, NX, NZ), f32),
            pltpu.VMEM((XW, BANDS, NZ), f32),
            pltpu.VMEM((XW, BANDS, NZ), f32),
            pltpu.VMEM((2, 16, 128), f32),
            pltpu.VMEM((16, 128), f32),
            pltpu.VMEM((2, 16, 128), f32),
            pltpu.VMEM((8, 16, 128), f32),
            pltpu.VMEM((8, 16, 128), f32),
            pltpu.VMEM((4, 16, 128), f32),
            dma((8,)),
            dma,
            dma((NG,)),
            dma,
            dma,
            dma((2,)),
            dma((2,)),
            dma((DEGREE, 2)),
            dma((DEGREE, 2)),
            dma,
            dma,
            dma((5,)),
            dma((5,)),
            dma,
            dma,
        ],
        compiler_params=pltpu.CompilerParams(collective_id=0, has_side_effects=True),
    )(start_bands, potential)


def solution(mesh):
    in_specs = (P("band", "gx", "gy", None), P("gx", "gy", None))
    out_specs = P("band", "gx", "gy", None)
    return jax.shard_map(on_device, mesh=mesh, in_specs=in_specs, out_specs=out_specs, check_vma=False)
```

time: 360 us -> 84.1 us (0.23)
  blocking collectives: 173 us -> 0 us
  waiting for transfers between devices: 93 us -> 0 us
  Pallas kernels: 0 us -> 82.4 us
  starting transfers between devices: 49.3 us -> 0 us
  other arithmetic: 17.4 us -> 0 us
  between operations: 14.1 us -> 0.01 us
  local copies, waits for them, and re-layouts: 8.21 us -> 1.62 us
  matrix products: 4.01 us -> 0 us
    psum x1 -> x0, blocking collectives: 131 us -> none  [on_device(): summed = lax.psum(products, ('gx', 'gy'))]
    pallas_call x0 -> x1, Pallas kernels: none -> 82.4 us  [on_device(): pl.pallas_call(kernel, out_shape=jax.ShapeDtypeStruct((8, XW, YW, NZ), f3...]
    ppermute x16 -> x0, waiting for transfers between devices: 50.3 us -> none  [the longest x8 30.6 us: padded_2(): lax.ppermute(lax.slice_in_dim(block, block.shape[dim] - width, None, axis...]
    ppermute x16 -> x0, starting transfers between devices: 49.3 us -> none  [the longest x8 24.6 us: padded_2(): lax.ppermute(lax.slice_in_dim(block, block.shape[dim] - width, None, axis...]
    all_gather x1 -> x0, waiting for transfers between devices: 42.7 us -> none  [on_device(): lax.all_gather(flattened, 'band', axis=0, tiled=True)]
    all_gather x1 -> x0, blocking collectives: 42.6 us -> none  [on_device(): lax.all_gather(summed, 'band', axis=0, tiled=True) * (1.0 / total_cells)]
    another operation x5 -> x0, other arithmetic: 12.1 us -> none  [the longest x3 6.52 us: invert_factor(): lower_factor = jnp.linalg.cholesky(margin)]
    slice x52 -> x0, local copies, waits for them, and re-layouts: 5.7 us -> none  [the longest x36 4.08 us: hamiltonian(): jnp.roll(field, offset, 3)]
  transfers between devices with their start and end apart: 17 -> 0, of which waited for: 13 -> 0; matrix products, arithmetic and copies ran while one was open for 2% -> 0% of each run, Pallas kernels for 0% -> 0%
where the time goes in v1:
time: 84.1 us; the launch traced here: 84 us
  Pallas kernels  82.4 us (98%)
  local copies, waits for them, and re-layouts  1.62 us (2%)
    pallas_call x1, Pallas kernels, on_device(): pl.pallas_call(kernel, out_shape=jax.ShapeDtypeStruct((8, XW, YW, NZ), f3...  82.4 us

profile of v1, /device:TPU:1, one launch (start us, length us, event | category | flops | bytes accessed | tf_op | source)
XLA Modules:
  0.0 84.0 jit_solution(6663743929828169831)
XLA Ops:
  0.0 82.4 %shard_map.28 = f32[8,6,8,128]{3,2,1,0:T(8,128)} custom-call(f32[8,6,8,128]{3,2,1,0:T(8,128)} %start.1, f32[6,8,128]{2,1,0:T(8,128)} %pot.1), custom_call_target="tpu_custom_call" | custom-call | tf_op jit(solution)/shard_map/pallas_call | solution.py:350
  82.4 1.6 %copy.4 = f32[8,6,8,128]{3,2,1,0:T(8,128)} copy(f32[8,6,8,128]{3,2,1,0:T(8,128)} %shard_map.28) | data formatting | bytes 393216

commit v2 on v1

v2 whole, which is shorter than its diff:
```python
import jax
import jax.numpy as jnp
from jax import lax
from jax.experimental import pallas as pl
from jax.experimental.pallas import tpu as pltpu
from jax.sharding import PartitionSpec as P

DEGREE = 4
COEFFS = (
    -5369.0 / 1800.0,
    12.0 / 7.0,
    -15.0 / 56.0,
    10.0 / 189.0,
    -1.0 / 112.0,
    2.0 / 1925.0,
    -1.0 / 16632.0,
)
LOWER_END = -0.5
CUT_LOW = 3.0
CUT_HIGH = 12.7
REACH = 6
MESH = pl.DeviceIdType.MESH
NB, NG, NY = 8, 8, 8
XW, YW, NX, NZ = 6, 8, 48, 128
BANDS = 64
CELLS = 48 * 64 * 128
CHUNKS = 3
PIECES = {2: (0, 4, 8), 3: (0, 3, 6, 8)}[CHUNKS]
GX_ORDER = (4, 5, 3, 2, 6, 7, 1)
BAND_ORDER = (4, 5, 3, 2, 6, 7, 1)
RING_ORDER = (4, 3, 5, 2, 6, 1, 7)


def filter_weights(degree):
    half_width = (CUT_HIGH - CUT_LOW) / 2.0
    middle = (CUT_HIGH + CUT_LOW) / 2.0
    sigma = half_width / (LOWER_END - middle)
    tau = 2.0 / sigma
    first = sigma / half_width
    others = []
    for index in range(degree - 1):
        sigma_new = 1.0 / (tau - sigma)
        others.append((2.0 * sigma_new / half_width, sigma * sigma_new))
        sigma = sigma_new
    return (middle, first, others)


def wait_bytes(ref, sem):
    pltpu.make_async_copy(ref, ref, sem).wait()


def dot(a, b, contract):
    return lax.dot_general(
        a,
        b,
        (contract, ((), ())),
        precision=lax.Precision.HIGHEST,
        preferred_element_type=jnp.float32,
    )


def inverse_factor(packed):
    wide = (8, 128)
    lane = lax.broadcasted_iota(jnp.int32, wide, 1)
    sub = lax.broadcasted_iota(jnp.int32, wide, 0)
    rows = []
    for t in range(8):
        part = packed[8 * (t % 4) : 8 * (t % 4) + 8]
        if t >= 4:
            part = pltpu.roll(part, 64, 1)
        unit = jnp.where(lane == sub + 8 * t, 1.0, 0.0)
        rows.append(jnp.where(lane >= 64, part, unit))
    for t in range(8):
        at = 64 + 8 * t
        row = [jnp.broadcast_to(rows[t][j : j + 1, :], wide) for j in range(8)]
        entry = {}
        for j in range(8):
            for l in range(j, 8):
                entry[j, l] = jnp.broadcast_to(rows[t][j : j + 1, at + l : at + l + 1], wide)
        column = {}
        for i in range(t + 1, 8):
            for j in range(8):
                column[i, j] = jnp.broadcast_to(rows[i][:, at + j : at + j + 1], wide)
        scaled = []
        for j in range(8):
            inverse = 1.0 / entry[j, j]
            scaled.append(row[j] * inverse)
            for l in range(j + 1, 8):
                factor = entry[j, l] * inverse
                row[l] = row[l] - factor * row[j]
                for m in range(l, 8):
                    entry[l, m] = entry[l, m] - factor * entry[j, m]
                for i in range(t + 1, 8):
                    column[i, l] = column[i, l] - column[i, j] * factor
        for i in range(t + 1, 8):
            for j in range(8):
                rows[i] = rows[i] - column[i, j] * scaled[j]
        for j in range(1, 8):
            rows[t] = jnp.where(sub == j, row[j], rows[t])
    done = []
    for t in range(8):
        pivots = jnp.sum(jnp.where(lane == sub + (8 * t + 64), rows[t], 0.0), axis=1, keepdims=True)
        done.append(rows[t] * (1.0 / jnp.sqrt(pivots)))
    return jnp.concatenate(done, axis=0)[:, :BANDS]


def kernel(
    start,
    pot,
    out,
    own,
    own_pot,
    turned,
    turned_pot,
    field,
    last,
    pots,
    acc,
    pencil,
    rotated,
    packed,
    half,
    sum_x,
    sum_y,
    sum_z,
    whole,
    local_sem,
    ax_send,
    ax_recv,
    pot_send,
    pot_recv,
    first_send,
    first_recv,
    halo_send,
    halo_recv,
    pen_send,
    pen_recv,
    sum_send,
    sum_recv,
    back_send,
    back_recv,
):
    b = lax.axis_index("band")
    g = lax.axis_index("gx")
    r = lax.axis_index("gy")

    def remote(src, dst, send, recv, device):
        copy = pltpu.make_async_remote_copy(
            src_ref=src, dst_ref=dst, send_sem=send, recv_sem=recv, device_id=device, device_id_type=MESH
        )
        copy.start()
        return copy

    load = pltpu.make_async_copy(start, own, local_sem.at[0])
    load.start()
    load_pot = pltpu.make_async_copy(pot, own_pot, local_sem.at[1])
    load_pot.start()

    plane_peers = [(db, dg) for db in range(NB) for dg in range(NG) if db or dg]
    plane_peers.sort(key=lambda pair: -(2 * min(pair[0] // 2, 4 - pair[0] // 2) + min(pair[1] // 2, 4 - pair[1] // 2)))
    barrier = pltpu.get_barrier_semaphore()
    for db, dg in plane_peers:
        device = {"band": lax.rem(b + db, NB), "gx": lax.rem(g + dg, NG)}
        pl.semaphore_signal(barrier, inc=1, device_id=device, device_id_type=MESH)
    for dy in range(1, NY):
        pl.semaphore_signal(barrier, inc=1, device_id={"gy": lax.rem(r + dy, NY)}, device_id_type=MESH)

    load.wait()
    for i in range(NG):
        for x in range(XW):
            turned[i, :, x, :] = own[i, x]
    load_pot.wait()
    for x in range(XW):
        turned_pot[:, x, :] = own_pot[x]
    pl.semaphore_wait(barrier, len(plane_peers) + NY - 1)

    slot = pl.ds(XW * g, XW)
    for dg in GX_ORDER:
        to = lax.rem(g + dg, NG)
        remote(turned.at[to], field.at[0, pl.ds(REACH, YW), slot, :], ax_send, ax_recv.at[g], {"gx": to})
    copy = pltpu.make_async_copy(turned.at[g], field.at[0, pl.ds(REACH, YW), slot, :], ax_recv.at[g])
    copy.start()
    for dg in GX_ORDER:
        to = lax.rem(g + dg, NG)
        remote(turned_pot, pots.at[:, slot, :], pot_send, pot_recv, {"gx": to})
    copy_pot = pltpu.make_async_copy(turned_pot, pots.at[:, slot, :], local_sem.at[2])
    copy_pot.start()

    up = {"gy": lax.rem(r + 1, NY)}
    down = {"gy": lax.rem(r + NY - 1, NY)}

    def halo(k, cols, send, recv):
        return [
            remote(
                field.at[k, pl.ds(YW, REACH), cols, :],
                field.at[k, pl.ds(0, REACH), cols, :],
                send(0),
                recv(0),
                up,
            ),
            remote(
                field.at[k, pl.ds(REACH, REACH), cols, :],
                field.at[k, pl.ds(YW + REACH, REACH), cols, :],
                send(1),
                recv(1),
                down,
            ),
        ]

    for c in range(CHUNKS):
        for source in range(PIECES[c], PIECES[c + 1]):
            cols = pl.ds(XW * source, XW)
            wait_bytes(field.at[0, pl.ds(REACH, YW), cols, :], ax_recv.at[source])
            halo(0, cols, lambda side: first_send.at[side], lambda side, c=c: first_recv.at[side, c])

    middle, first, others = filter_weights(DEGREE)
    width = NX // CHUNKS
    moves = []
    for k in range(DEGREE):
        scale = first if k == 0 else others[k - 1][0]
        weights = [-0.5 * c * scale for c in COEFFS]

        def local_part(y, carry, k=k, scale=scale, weights=weights):
            plane = field[k, REACH + y]
            total = (3.0 * weights[0] - middle * scale) * plane
            for j in range(1, REACH + 1):
                near = pltpu.roll(plane, j, 0) + pltpu.roll(plane, NX - j, 0)
                near = near + pltpu.roll(plane, j, 1) + pltpu.roll(plane, NZ - j, 1)
                total = total + weights[j] * near
            if k:
                total = total + scale * pots[y] * plane
                total = total - others[k - 1][1] * field[k - 1, REACH + y]
            acc[y] = total
            return carry

        lax.fori_loop(0, YW, local_part, 0)
        if k == 0:
            copy_pot.wait()
            wait_bytes(pots.at[:, pl.ds(0, XW * (NG - 1)), :], pot_recv)
        for y in range(YW):
            total = acc[y]
            if k == 0:
                total = total + scale * pots[y] * field[k, REACH + y]
            for j in range(1, REACH + 1):
                if y - j >= 0:
                    total = total + weights[j] * field[k, REACH + y - j]
                if y + j < YW:
                    total = total + weights[j] * field[k, REACH + y + j]
            acc[y] = total

        later = []
        for c in range(CHUNKS):
            low, high = width * c, width * (c + 1)
            cols = pl.ds(low, width)
            for side in range(2):
                if k:
                    moves[c][side].wait()
                else:
                    got = pl.ds(XW * PIECES[c], XW * (PIECES[c + 1] - PIECES[c]))
                    wait_bytes(field.at[0, pl.ds((YW + REACH) * side, REACH), got, :], first_recv.at[side, c])
            for y in range(YW):
                total = acc[y, low:high]
                for j in range(1, REACH + 1):
                    if y - j < 0:
                        total = total + weights[j] * field[k, REACH + y - j, low:high]
                    if y + j >= YW:
                        total = total + weights[j] * field[k, REACH + y + j, low:high]
                if k < DEGREE - 1:
                    field[k + 1, REACH + y, low:high] = total
                else:
                    last[y, low:high] = total
            if k < DEGREE - 1:
                later.append(
                    halo(
                        k + 1,
                        cols,
                        lambda side, k=k, c=c: halo_send.at[k + 1, side, c],
                        lambda side, k=k, c=c: halo_recv.at[k + 1, side, c],
                    )
                )
        moves = later

    band = NG * b + g
    for db, dg in plane_peers:
        to_b = lax.rem(b + db, NB)
        to_g = lax.rem(g + dg, NG)
        remote(
            last.at[to_b, pl.ds(XW * to_g, XW), :],
            pencil.at[:, band, :],
            pen_send,
            pen_recv,
            {"band": to_b, "gx": to_g},
        )
    copy = pltpu.make_async_copy(last.at[b, pl.ds(XW * g, XW), :], pencil.at[:, band, :], local_sem.at[0])
    copy.start()
    copy.wait()
    wait_bytes(own.at[pl.ds(0, NG - 1)], ax_send)
    wait_bytes(own.at[pl.ds(0, NG - 1)], pot_send)
    for side in range(2):
        wait_bytes(field.at[0, pl.ds((YW + REACH) * side, REACH)], first_send.at[side])
    wait_bytes(pencil.at[:, pl.ds(0, BANDS - 1), :], pen_recv)

    cells = jnp.concatenate([pencil[x] for x in range(XW)], axis=1)
    twice = jnp.concatenate([cells, cells], axis=0)
    products = dot(cells, twice, ((1,), (1,)))
    lane = lax.broadcasted_iota(jnp.int32, (32, 128), 1)
    joined = jnp.where(lane < 64, products[32:], products[:32])
    packed[0] = joined[:16]
    packed[1] = joined[16:]

    core = lax.rem(b, 2)
    zhi, zlo, chip_x = b // 2, lax.rem(g, 2), g // 2
    place = 2 * zhi + zlo
    partner = {"band": b + 1 - 2 * core}

    def along(index, first_axis):
        return {
            "band": (1 - first_axis) * b + first_axis * (2 * (index // 2) + core),
            "gx": (1 - first_axis) * g + first_axis * (2 * chip_x + lax.rem(index, 2)),
            "gy": (1 - first_axis) * index + first_axis * r,
        }

    def spread(table, value, index, stage, offsets, device_of):
        count = len(offsets)
        table[index] = value
        for d in offsets:
            remote(
                table.at[index],
                table.at[index],
                sum_send.at[stage],
                sum_recv.at[stage],
                device_of(lax.rem(index + d, count + 1)),
            )
        wait_bytes(table.at[pl.ds(0, count)], sum_recv.at[stage])
        parts = [table[i] for i in range(count + 1)]
        while len(parts) > 1:
            parts = [parts[i] + parts[i + 1] for i in range(0, len(parts), 2)]
        return parts[0]

    remote(packed.at[1 - core], half, sum_send.at[0], sum_recv.at[0], partner)
    wait_bytes(half, sum_recv.at[0])
    value = packed[core] + half[...]
    value = spread(sum_x, value, chip_x, 1, (2, 1, 3), lambda i: {"gx": 2 * i + zlo})
    mine = (1 - core) * r + core * place
    value = spread(sum_y, value, mine, 2, RING_ORDER, lambda i: along(i, core))
    mine = (1 - core) * place + core * r
    value = spread(sum_z, value, mine, 3, RING_ORDER, lambda i: along(i, 1 - core))
    whole[core] = value * (1.0 / CELLS)
    remote(whole.at[core], whole.at[core], sum_send.at[4], sum_recv.at[4], partner)
    wait_bytes(half, sum_recv.at[4])

    inverse = inverse_factor(whole[...].reshape(32, 128))
    for x in range(XW):
        turn = dot(inverse, pencil[x], ((1,), (0,)))
        for i in range(NB):
            rotated[i, :, x, :] = turn[8 * i : 8 * i + 8]

    for db in BAND_ORDER:
        to = lax.rem(b + db, NB)
        remote(rotated.at[to], out.at[:, :, b, :], back_send, back_recv, {"band": to})
    copy = pltpu.make_async_copy(rotated.at[b], out.at[:, :, b, :], local_sem.at[1])
    copy.start()
    wait_bytes(pencil.at[:, pl.ds(0, BANDS - 1), :], pen_send)
    for stage, table in ((1, sum_x.at[pl.ds(0, 3)]), (2, sum_y.at[pl.ds(0, 7)]), (3, sum_z.at[pl.ds(0, 7)])):
        wait_bytes(table, sum_send.at[stage])
    wait_bytes(half, sum_send.at[0])
    wait_bytes(half, sum_send.at[4])
    copy.wait()
    wait_bytes(own.at[pl.ds(0, NB - 1)], back_recv)
    wait_bytes(own.at[pl.ds(0, NB - 1)], back_send)


def on_device(start_bands, potential):
    f32 = jnp.float32
    dma = pltpu.SemaphoreType.DMA
    return pl.pallas_call(
        kernel,
        out_shape=jax.ShapeDtypeStruct((8, XW, YW, NZ), f32),
        in_specs=[pl.BlockSpec(memory_space=pl.ANY)] * 2,
        out_specs=pl.BlockSpec(memory_space=pl.ANY),
        scratch_shapes=[
            pltpu.VMEM((8, XW, YW, NZ), f32),
            pltpu.VMEM((XW, YW, NZ), f32),
            pltpu.VMEM((8, YW, XW, NZ), f32),
            pltpu.VMEM((YW, XW, NZ), f32),
            pltpu.VMEM((DEGREE, YW + 2 * REACH, NX, NZ), f32),
            pltpu.VMEM((YW, NX, NZ), f32),
            pltpu.VMEM((YW, NX, NZ), f32),
            pltpu.VMEM((YW, NX, NZ), f32),
            pltpu.VMEM((XW, BANDS, NZ), f32),
            pltpu.VMEM((NB, 8, XW, NZ), f32),
            pltpu.VMEM((2, 16, 128), f32),
            pltpu.VMEM((16, 128), f32),
            pltpu.VMEM((4, 16, 128), f32),
            pltpu.VMEM((8, 16, 128), f32),
            pltpu.VMEM((8, 16, 128), f32),
            pltpu.VMEM((2, 16, 128), f32),
            dma((3,)),
            dma,
            dma((NG,)),
            dma,
            dma,
            dma((2,)),
            dma((2, CHUNKS)),
            dma((DEGREE, 2, CHUNKS)),
            dma((DEGREE, 2, CHUNKS)),
            dma,
            dma,
            dma((5,)),
            dma((5,)),
            dma,
            dma,
        ],
        compiler_params=pltpu.CompilerParams(collective_id=0, has_side_effects=True),
    )(start_bands, potential)


def solution(mesh):
    in_specs = (P("band", "gx", "gy", None), P("gx", "gy", None))
    out_specs = P("band", "gx", "gy", None)
    return jax.shard_map(on_device, mesh=mesh, in_specs=in_specs, out_specs=out_specs, check_vma=False)
```

time: 84.1 us -> 72.9 us (0.87)
  Pallas kernels: 82.4 us -> 71.2 us
    pallas_call x1, Pallas kernels: 82.4 us -> 71.2 us  [on_device(): pl.pallas_call(kernel, out_shape=jax.ShapeDtypeStruct((8, XW, YW, NZ), f3...]
where the time goes in v2:
time: 72.9 us; the launch traced here: 72.8 us
  Pallas kernels  71.2 us (98%)
  local copies, waits for them, and re-layouts  1.62 us (2%)
    pallas_call x1, Pallas kernels, on_device(): pl.pallas_call(kernel, out_shape=jax.ShapeDtypeStruct((8, XW, YW, NZ), f3...  71.2 us
    unnamed x1, local copies, waits for them, and re-layouts  1.62 us

profile of v2, /device:TPU:1, one launch (start us, length us, event | category | flops | bytes accessed | tf_op | source)
XLA Modules:
  0.0 72.8 jit_solution(1261954117526009023)
XLA Ops:
  0.0 71.2 %shard_map.28 = f32[8,6,8,128]{3,2,1,0:T(8,128)} custom-call(f32[8,6,8,128]{3,2,1,0:T(8,128)} %start.1, f32[6,8,128]{2,1,0:T(8,128)} %pot.1), custom_call_target="tpu_custom_call" | custom-call | tf_op jit(solution)/shard_map/pallas_call | solution.py:376
  71.2 1.6 %copy.4 = f32[8,6,8,128]{3,2,1,0:T(8,128)} copy(f32[8,6,8,128]{3,2,1,0:T(8,128)} %shard_map.28) | data formatting | bytes 393216

commit v3 on v2

--- a/solution.py
+++ b/solution.py
@@ -119,11 +119,10 @@
     pencil,
     rotated,
     packed,
-    half,
     sum_x,
     sum_y,
-    sum_z,
     whole,
+    ready,
     local_sem,
     ax_send,
     ax_recv,
@@ -159,11 +158,15 @@
     plane_peers = [(db, dg) for db in range(NB) for dg in range(NG) if db or dg]
     plane_peers.sort(key=lambda pair: -(2 * min(pair[0] // 2, 4 - pair[0] // 2) + min(pair[1] // 2, 4 - pair[1] // 2)))
     barrier = pltpu.get_barrier_semaphore()
-    for db, dg in plane_peers:
-        device = {"band": lax.rem(b + db, NB), "gx": lax.rem(g + dg, NG)}
+    core = lax.rem(b, 2)
+    zhi, zlo, chip_x = b // 2, lax.rem(g, 2), g // 2
+    partner = {"band": b + 1 - 2 * core}
+    beside = [{"band": lax.rem(b + db, NB)} for db in (2, NB - 2)]
+    greeted = beside + [partner]
+    greeted += [{"gx": lax.rem(g + dg, NG)} for dg in GX_ORDER]
+    greeted += [{"gy": lax.rem(r + dy, NY)} for dy in (1, NY - 1)]
+    for device in greeted:
         pl.semaphore_signal(barrier, inc=1, device_id=device, device_id_type=MESH)
-    for dy in range(1, NY):
-        pl.semaphore_signal(barrier, inc=1, device_id={"gy": lax.rem(r + dy, NY)}, device_id_type=MESH)
 
     load.wait()
     for i in range(NG):
@@ -172,7 +175,7 @@
     load_pot.wait()
     for x in range(XW):
         turned_pot[:, x, :] = own_pot[x]
-    pl.semaphore_wait(barrier, len(plane_peers) + NY - 1)
+    pl.semaphore_wait(barrier, len(greeted))
 
     slot = pl.ds(XW * g, XW)
     for dg in GX_ORDER:
@@ -180,11 +183,6 @@
         remote(turned.at[to], field.at[0, pl.ds(REACH, YW), slot, :], ax_send, ax_recv.at[g], {"gx": to})
     copy = pltpu.make_async_copy(turned.at[g], field.at[0, pl.ds(REACH, YW), slot, :], ax_recv.at[g])
     copy.start()
-    for dg in GX_ORDER:
-        to = lax.rem(g + dg, NG)
-        remote(turned_pot, pots.at[:, slot, :], pot_send, pot_recv, {"gx": to})
-    copy_pot = pltpu.make_async_copy(turned_pot, pots.at[:, slot, :], local_sem.at[2])
-    copy_pot.start()
 
     up = {"gy": lax.rem(r + 1, NY)}
     down = {"gy": lax.rem(r + NY - 1, NY)}
@@ -213,41 +211,67 @@
             wait_bytes(field.at[0, pl.ds(REACH, YW), cols, :], ax_recv.at[source])
             halo(0, cols, lambda side: first_send.at[side], lambda side, c=c: first_recv.at[side, c])
 
+    for dg in GX_ORDER:
+        to = lax.rem(g + dg, NG)
+        remote(turned_pot, pots.at[:, slot, :], pot_send, pot_recv, {"gx": to})
+    copy_pot = pltpu.make_async_copy(turned_pot, pots.at[:, slot, :], local_sem.at[2])
+    copy_pot.start()
+
+    def tell(devices, round_):
+        for device in devices:
+            pl.semaphore_signal(ready.at[round_], inc=1, device_id=device, device_id_type=MESH)
+
+    tell(beside, 0)
+
     middle, first, others = filter_weights(DEGREE)
     width = NX // CHUNKS
-    moves = []
+    factors = []
     for k in range(DEGREE):
         scale = first if k == 0 else others[k - 1][0]
-        weights = [-0.5 * c * scale for c in COEFFS]
-
-        def local_part(y, carry, k=k, scale=scale, weights=weights):
-            plane = field[k, REACH + y]
+        factors.append((scale, [-0.5 * c * scale for c in COEFFS]))
+
+    def side_part(k, low, high):
+        scale, weights = factors[k]
+        for y in range(YW):
+            plane = field[k, REACH + y, low:high]
             total = (3.0 * weights[0] - middle * scale) * plane
+            if k:
+                total = total + scale * pots[y, low:high] * plane
+                total = total - others[k - 1][1] * field[k - 1, REACH + y, low:high]
             for j in range(1, REACH + 1):
-                near = pltpu.roll(plane, j, 0) + pltpu.roll(plane, NX - j, 0)
-                near = near + pltpu.roll(plane, j, 1) + pltpu.roll(plane, NZ - j, 1)
+                near = pltpu.roll(plane, j, 1) + pltpu.roll(plane, NZ - j, 1)
+                if y - j >= 0:
+                    near = near + field[k, REACH + y - j, low:high]
+                if y + j < YW:
+                    near = near + field[k, REACH + y + j, low:high]
                 total = total + weights[j] * near
-            if k:
-                total = total + scale * pots[y] * plane
-                total = total - others[k - 1][1] * field[k - 1, REACH + y]
-            acc[y] = total
+            acc[y, low:high] = total
+
+    def x_part(k):
+        weights = factors[k][1]
+
+        def planes(i, carry):
+            for y in (2 * i, 2 * i + 1):
+                plane = field[k, REACH + y]
+                total = acc[y]
+                for j in range(1, REACH + 1):
+                    total = total + weights[j] * (pltpu.roll(plane, j, 0) + pltpu.roll(plane, NX - j, 0))
+                acc[y] = total
             return carry
 
-        lax.fori_loop(0, YW, local_part, 0)
+        lax.fori_loop(0, YW // 2, planes, 0)
+
+    moves = []
+    for c in range(CHUNKS):
+        side_part(0, width * c, width * (c + 1))
+    for k in range(DEGREE):
+        scale, weights = factors[k]
+        x_part(k)
         if k == 0:
             copy_pot.wait()
             wait_bytes(pots.at[:, pl.ds(0, XW * (NG - 1)), :], pot_recv)
-        for y in range(YW):
-            total = acc[y]
-            if k == 0:
-                total = total + scale * pots[y] * field[k, REACH + y]
-            for j in range(1, REACH + 1):
-                if y - j >= 0:
-                    total = total + weights[j] * field[k, REACH + y - j]
-                if y + j < YW:
-                    total = total + weights[j] * field[k, REACH + y + j]
-            acc[y] = total
-
+            for y in range(YW):
+                acc[y] = acc[y] + scale * pots[y] * field[0, REACH + y]
         later = []
         for c in range(CHUNKS):
             low, high = width * c, width * (c + 1)
@@ -278,8 +302,16 @@
                         lambda side, k=k, c=c: halo_recv.at[k + 1, side, c],
                     )
                 )
+                side_part(k + 1, low, high)
         moves = later
-
+        if k == 0:
+            pl.semaphore_wait(ready.at[0], len(beside))
+            tell([partner], 1)
+        if k == 1:
+            pl.semaphore_wait(ready.at[1], 1)
+            tell([{"gx": lax.rem(g + dg, NG)} for dg in GX_ORDER], 2)
+
+    pl.semaphore_wait(ready.at[2], NG - 1)
     band = NG * b + g
     for db, dg in plane_peers:
         to_b = lax.rem(b + db, NB)
@@ -308,48 +340,53 @@
     packed[0] = joined[:16]
     packed[1] = joined[16:]
 
-    core = lax.rem(b, 2)
-    zhi, zlo, chip_x = b // 2, lax.rem(g, 2), g // 2
+    piece = 2 * chip_x + core
     place = 2 * zhi + zlo
-    partner = {"band": b + 1 - 2 * core}
-
-    def along(index, first_axis):
-        return {
-            "band": (1 - first_axis) * b + first_axis * (2 * (index // 2) + core),
-            "gx": (1 - first_axis) * g + first_axis * (2 * chip_x + lax.rem(index, 2)),
-            "gy": (1 - first_axis) * index + first_axis * r,
-        }
-
-    def spread(table, value, index, stage, offsets, device_of):
-        count = len(offsets)
-        table[index] = value
-        for d in offsets:
-            remote(
-                table.at[index],
-                table.at[index],
-                sum_send.at[stage],
-                sum_recv.at[stage],
-                device_of(lax.rem(index + d, count + 1)),
-            )
-        wait_bytes(table.at[pl.ds(0, count)], sum_recv.at[stage])
-        parts = [table[i] for i in range(count + 1)]
+
+    def added(table, start_at=0):
+        parts = [table[start_at + i] for i in range(8)]
         while len(parts) > 1:
             parts = [parts[i] + parts[i + 1] for i in range(0, len(parts), 2)]
         return parts[0]
 
-    remote(packed.at[1 - core], half, sum_send.at[0], sum_recv.at[0], partner)
-    wait_bytes(half, sum_recv.at[0])
-    value = packed[core] + half[...]
-    value = spread(sum_x, value, chip_x, 1, (2, 1, 3), lambda i: {"gx": 2 * i + zlo})
+    def along(index, axis, to_core):
+        return {
+            "band": 2 * ((1 - axis) * zhi + axis * (index // 2)) + to_core,
+            "gx": (1 - axis) * g + axis * (2 * chip_x + lax.rem(index, 2)),
+            "gy": (1 - axis) * index + axis * r,
+        }
+
+    for d in GX_ORDER:
+        other = lax.rem(piece + d, 8)
+        to_core = lax.rem(other, 2)
+        remote(
+            packed.at[to_core],
+            sum_x.at[piece],
+            sum_send.at[0],
+            sum_recv.at[0],
+            {"band": 2 * zhi + to_core, "gx": 2 * (other // 2) + zlo},
+        )
+    sum_x[piece] = packed[core]
+    wait_bytes(sum_x.at[pl.ds(0, 7)], sum_recv.at[0])
+
     mine = (1 - core) * r + core * place
-    value = spread(sum_y, value, mine, 2, RING_ORDER, lambda i: along(i, core))
+    sum_y[mine] = added(sum_x)
+    for d in RING_ORDER:
+        to = along(lax.rem(mine + d, 8), core, core)
+        remote(sum_y.at[mine], sum_y.at[mine], sum_send.at[1], sum_recv.at[1], to)
+    wait_bytes(sum_y.at[pl.ds(0, 7)], sum_recv.at[1])
+
     mine = (1 - core) * place + core * r
-    value = spread(sum_z, value, mine, 3, RING_ORDER, lambda i: along(i, 1 - core))
-    whole[core] = value * (1.0 / CELLS)
-    remote(whole.at[core], whole.at[core], sum_send.at[4], sum_recv.at[4], partner)
-    wait_bytes(half, sum_recv.at[4])
-
-    inverse = inverse_factor(whole[...].reshape(32, 128))
+    row = 8 * core + mine
+    whole[row] = added(sum_y)
+    for d in RING_ORDER + (0,):
+        for to_core in (1 - core, core)[: 2 if d else 1]:
+            to = along(lax.rem(mine + d, 8), 1 - core, to_core)
+            remote(whole.at[row], whole.at[row], sum_send.at[2], sum_recv.at[2], to)
+    wait_bytes(whole.at[pl.ds(0, 15)], sum_recv.at[2])
+    margin = jnp.concatenate([added(whole, 0), added(whole, 8)], axis=0) * (1.0 / CELLS)
+
+    inverse = inverse_factor(margin)
     for x in range(XW):
         turn = dot(inverse, pencil[x], ((1,), (0,)))
         for i in range(NB):
@@ -361,10 +398,8 @@
     copy = pltpu.make_async_copy(rotated.at[b], out.at[:, :, b, :], local_sem.at[1])
     copy.start()
     wait_bytes(pencil.at[:, pl.ds(0, BANDS - 1), :], pen_send)
-    for stage, table in ((1, sum_x.at[pl.ds(0, 3)]), (2, sum_y.at[pl.ds(0, 7)]), (3, sum_z.at[pl.ds(0, 7)])):
+    for stage, table in enumerate((sum_x.at[pl.ds(0, 7)], sum_y.at[pl.ds(0, 7)], whole.at[pl.ds(0, 15)])):
         wait_bytes(table, sum_send.at[stage])
-    wait_bytes(half, sum_send.at[0])
-    wait_bytes(half, sum_send.at[4])
     copy.wait()
     wait_bytes(own.at[pl.ds(0, NB - 1)], back_recv)
     wait_bytes(own.at[pl.ds(0, NB - 1)], back_send)
@@ -390,11 +425,10 @@
             pltpu.VMEM((XW, BANDS, NZ), f32),
             pltpu.VMEM((NB, 8, XW, NZ), f32),
             pltpu.VMEM((2, 16, 128), f32),
-            pltpu.VMEM((16, 128), f32),
-            pltpu.VMEM((4, 16, 128), f32),
             pltpu.VMEM((8, 16, 128), f32),
             pltpu.VMEM((8, 16, 128), f32),
-            pltpu.VMEM((2, 16, 128), f32),
+            pltpu.VMEM((16, 16, 128), f32),
+            pltpu.SemaphoreType.REGULAR((3,)),
             dma((3,)),
             dma,
             dma((NG,)),
@@ -406,13 +440,15 @@
             dma((DEGREE, 2, CHUNKS)),
             dma,
             dma,
-            dma((5,)),
-            dma((5,)),
+            dma((3,)),
+            dma((3,)),
             dma,
             dma,
         ],
-        compiler_params=pltpu.CompilerParams(collective_id=0, has_side_effects=True),
-    )(start_bands, potential)
+        compiler_params=pltpu.CompilerParams(
+            collective_id=0, has_side_effects=True, vmem_limit_bytes=24 * 1024 * 1024
+        ),
+    )(*[pltpu.with_memory_space_constraint(value, pltpu.HBM) for value in (start_bands, potential)])
 
 
 def solution(mesh):

time: 72.9 us -> 67.9 us (0.931)
  Pallas kernels: 71.2 us -> 67.1 us
  local copies, waits for them, and re-layouts: 1.62 us -> 0.68 us
    pallas_call x1, Pallas kernels: 71.2 us -> 67.1 us  [on_device(): pl.pallas_call(kernel, out_shape=jax.ShapeDtypeStruct((8, XW, YW, NZ), f3...]
    unnamed x1, local copies, waits for them, and re-layouts: 1.62 us -> 0.68 us
where the time goes in v3:
time: 67.9 us; the launch traced here: 67.8 us
  Pallas kernels  67.1 us (99%)
  local copies, waits for them, and re-layouts  0.68 us (1%)
    pallas_call x1, Pallas kernels, on_device(): pl.pallas_call(kernel, out_shape=jax.ShapeDtypeStruct((8, XW, YW, NZ), f3...  67.1 us

profile of v3, /device:TPU:1, one launch (start us, length us, event | category | flops | bytes accessed | tf_op | source)
XLA Modules:
  0.0 67.8 jit_solution(10543024943235874278)
XLA Ops:
  0.0 67.1 %shard_map.28 = f32[8,6,8,128]{3,2,1,0:T(8,128)S(1)} custom-call(f32[8,6,8,128]{3,2,1,0:T(8,128)} %start.1, f32[6,8,128]{2,1,0:T(8,128)} %pot.1), custom_call_target="tpu_custom_call" | custom-call | tf_op jit(solution)/shard_map/pallas_call | solution.py:411
  67.1 0.7 %copy.4 = f32[8,6,8,128]{3,2,1,0:T(8,128)} copy(f32[8,6,8,128]{3,2,1,0:T(8,128)S(1)} %shard_map.28) | data formatting | bytes 393216

commit v4 on v3

--- a/solution.py
+++ b/solution.py
@@ -155,8 +155,6 @@
     load_pot = pltpu.make_async_copy(pot, own_pot, local_sem.at[1])
     load_pot.start()
 
-    plane_peers = [(db, dg) for db in range(NB) for dg in range(NG) if db or dg]
-    plane_peers.sort(key=lambda pair: -(2 * min(pair[0] // 2, 4 - pair[0] // 2) + min(pair[1] // 2, 4 - pair[1] // 2)))
     barrier = pltpu.get_barrier_semaphore()
     core = lax.rem(b, 2)
     zhi, zlo, chip_x = b // 2, lax.rem(g, 2), g // 2
@@ -260,6 +258,26 @@
             return carry
 
         lax.fori_loop(0, YW // 2, planes, 0)
+
+    band = NG * b + g
+
+    def pass_on(to_g):
+        for db in BAND_ORDER + (0,):
+            to_b = lax.rem(b + db, NB)
+            src = last.at[to_b, pl.ds(XW * to_g, XW), :]
+            dst = pencil.at[:, band, :]
+
+            def send(src=src, dst=dst, to_b=to_b):
+                remote(src, dst, pen_send, pen_recv, {"band": to_b, "gx": to_g})
+
+            if db:
+                send()
+            else:
+                pl.when(g != to_g)(send)
+
+                @pl.when(g == to_g)
+                def _(src=src, dst=dst):
+                    pltpu.make_async_copy(src, dst, local_sem.at[0]).start()
 
     moves = []
     for c in range(CHUNKS):
@@ -303,6 +321,11 @@
                     )
                 )
                 side_part(k + 1, low, high)
+            else:
+                if c == 0:
+                    pl.semaphore_wait(ready.at[2], NG - 1)
+                for to_g in range(low // XW, high // XW):
+                    pass_on(to_g)
         moves = later
         if k == 0:
             pl.semaphore_wait(ready.at[0], len(beside))
@@ -311,21 +334,7 @@
             pl.semaphore_wait(ready.at[1], 1)
             tell([{"gx": lax.rem(g + dg, NG)} for dg in GX_ORDER], 2)
 
-    pl.semaphore_wait(ready.at[2], NG - 1)
-    band = NG * b + g
-    for db, dg in plane_peers:
-        to_b = lax.rem(b + db, NB)
-        to_g = lax.rem(g + dg, NG)
-        remote(
-            last.at[to_b, pl.ds(XW * to_g, XW), :],
-            pencil.at[:, band, :],
-            pen_send,
-            pen_recv,
-            {"band": to_b, "gx": to_g},
-        )
-    copy = pltpu.make_async_copy(last.at[b, pl.ds(XW * g, XW), :], pencil.at[:, band, :], local_sem.at[0])
-    copy.start()
-    copy.wait()
+    wait_bytes(pencil.at[:, 0, :], local_sem.at[0])
     wait_bytes(own.at[pl.ds(0, NG - 1)], ax_send)
     wait_bytes(own.at[pl.ds(0, NG - 1)], pot_send)
     for side in range(2):

time: 67.9 us -> 67.7 us (level)
  no operation moved by 1% of the time
where the time goes in v4:
time: 67.7 us; the launch traced here: 67.6 us
  Pallas kernels  66.9 us (99%)
  local copies, waits for them, and re-layouts  0.68 us (1%)
    pallas_call x1, Pallas kernels, on_device(): pl.pallas_call(kernel, out_shape=jax.ShapeDtypeStruct((8, XW, YW, NZ), f3...  66.9 us

profile of v4, /device:TPU:1, one launch (start us, length us, event | category | flops | bytes accessed | tf_op | source)
XLA Modules:
  0.0 67.6 jit_solution(8300661317683429686)
XLA Ops:
  0.0 66.9 %shard_map.28 = f32[8,6,8,128]{3,2,1,0:T(8,128)S(1)} custom-call(f32[8,6,8,128]{3,2,1,0:T(8,128)} %start.1, f32[6,8,128]{2,1,0:T(8,128)} %pot.1), custom_call_target="tpu_custom_call" | custom-call | tf_op jit(solution)/shard_map/pallas_call | solution.py:420
  66.9 0.7 %copy.4 = f32[8,6,8,128]{3,2,1,0:T(8,128)} copy(f32[8,6,8,128]{3,2,1,0:T(8,128)S(1)} %shard_map.28) | data formatting | bytes 393216

commit v5 on v4

--- a/solution.py
+++ b/solution.py
@@ -261,13 +261,13 @@
 
     band = NG * b + g
 
-    def pass_on(to_g):
-        for db in BAND_ORDER + (0,):
+    def pass_on(targets):
+        for db, to_g in [(db, to_g) for db in BAND_ORDER + (0,) for to_g in targets]:
             to_b = lax.rem(b + db, NB)
             src = last.at[to_b, pl.ds(XW * to_g, XW), :]
             dst = pencil.at[:, band, :]
 
-            def send(src=src, dst=dst, to_b=to_b):
+            def send(src=src, dst=dst, to_b=to_b, to_g=to_g):
                 remote(src, dst, pen_send, pen_recv, {"band": to_b, "gx": to_g})
 
             if db:
@@ -324,8 +324,7 @@
             else:
                 if c == 0:
                     pl.semaphore_wait(ready.at[2], NG - 1)
-                for to_g in range(low // XW, high // XW):
-                    pass_on(to_g)
+                pass_on(range(low // XW, high // XW))
         moves = later
         if k == 0:
             pl.semaphore_wait(ready.at[0], len(beside))
@@ -396,20 +395,24 @@
     margin = jnp.concatenate([added(whole, 0), added(whole, 8)], axis=0) * (1.0 / CELLS)
 
     inverse = inverse_factor(margin)
-    for x in range(XW):
-        turn = dot(inverse, pencil[x], ((1,), (0,)))
-        for i in range(NB):
-            rotated[i, :, x, :] = turn[8 * i : 8 * i + 8]
-
-    for db in BAND_ORDER:
-        to = lax.rem(b + db, NB)
-        remote(rotated.at[to], out.at[:, :, b, :], back_send, back_recv, {"band": to})
-    copy = pltpu.make_async_copy(rotated.at[b], out.at[:, :, b, :], local_sem.at[1])
-    copy.start()
+    copies = []
+    for part in range(2):
+        for x in range(3):
+            turn = dot(inverse, pencil[3 * part + x], ((1,), (0,)))
+            for i in range(NB):
+                rotated[part, i, :, x, :] = turn[8 * i : 8 * i + 8]
+        there = pl.ds(3 * part, 3)
+        for db in BAND_ORDER:
+            to = lax.rem(b + db, NB)
+            remote(rotated.at[part, to], out.at[:, there, b, :], back_send, back_recv, {"band": to})
+        copy = pltpu.make_async_copy(rotated.at[part, b], out.at[:, there, b, :], local_sem.at[1 + part])
+        copy.start()
+        copies.append(copy)
     wait_bytes(pencil.at[:, pl.ds(0, BANDS - 1), :], pen_send)
     for stage, table in enumerate((sum_x.at[pl.ds(0, 7)], sum_y.at[pl.ds(0, 7)], whole.at[pl.ds(0, 15)])):
         wait_bytes(table, sum_send.at[stage])
-    copy.wait()
+    for copy in copies:
+        copy.wait()
     wait_bytes(own.at[pl.ds(0, NB - 1)], back_recv)
     wait_bytes(own.at[pl.ds(0, NB - 1)], back_send)
 
@@ -432,7 +435,7 @@
             pltpu.VMEM((YW, NX, NZ), f32),
             pltpu.VMEM((YW, NX, NZ), f32),
             pltpu.VMEM((XW, BANDS, NZ), f32),
-            pltpu.VMEM((NB, 8, XW, NZ), f32),
+            pltpu.VMEM((2, NB, 8, 3, NZ), f32),
             pltpu.VMEM((2, 16, 128), f32),
             pltpu.VMEM((8, 16, 128), f32),
             pltpu.VMEM((8, 16, 128), f32),

time: 67.7 us -> 67.6 us (level)
  no operation moved by 1% of the time
where the time goes in v5:
time: 67.6 us; the launch traced here: 67.4 us
  Pallas kernels  66.7 us (99%)
  local copies, waits for them, and re-layouts  0.68 us (1%)
    pallas_call x1, Pallas kernels, on_device(): pl.pallas_call(kernel, out_shape=jax.ShapeDtypeStruct((8, XW, YW, NZ), f3...  66.7 us

profile of v5, /device:TPU:1, one launch (start us, length us, event | category | flops | bytes accessed | tf_op | source)
XLA Modules:
  0.0 67.4 jit_solution(296083718013530355)
XLA Ops:
  0.0 66.7 %shard_map.28 = f32[8,6,8,128]{3,2,1,0:T(8,128)S(1)} custom-call(f32[8,6,8,128]{3,2,1,0:T(8,128)} %start.1, f32[6,8,128]{2,1,0:T(8,128)} %pot.1), custom_call_target="tpu_custom_call" | custom-call | tf_op jit(solution)/shard_map/pallas_call | solution.py:423
  66.8 0.7 %copy.4 = f32[8,6,8,128]{3,2,1,0:T(8,128)} copy(f32[8,6,8,128]{3,2,1,0:T(8,128)S(1)} %shard_map.28) | data formatting | bytes 393216
